TPU v7x, 32 devices: a whole 2x2x4 slice. The times are simulated.
32 devices in a mesh: sec: 2 (over x), gx: 4 (over y, core), gy: 4 (over z).
Axes of the slice: x: 2, y: 2, z: 4, core: 2. Of those that a mesh axis runs over, the one named last changes fastest.
Arguments:
- pressure: float32 [50, 128, 512], P(None, ('sec', 'gx'), 'gy'), may hold values from -4 to 4
- pressure_old: float32 [50, 128, 512], P(None, ('sec', 'gx'), 'gy'), may hold values from -4 to 4
- conductivity: float32 [50, 128, 512], P(None, ('sec', 'gx'), 'gy'), may hold values from 0.3 to 3
- vg_alpha: float32 [50, 128, 512], P(None, ('sec', 'gx'), 'gy'), may hold values from 0.5 to 4
- porosity: float32 [50, 128, 512], P(None, ('sec', 'gx'), 'gy'), may hold values from 0.3 to 0.5
- land_mask: int32 [128, 512], P(('sec', 'gx'), 'gy'), may hold values 0 or 1
- nitrate: float32 [10, 8192], P(None, ('sec', 'gx', 'gy')), may hold values from 0.5 to 2
- patch_column: int32 [8192], P(('sec', 'gx', 'gy')), may hold values from 0 to 2047
- crop_type: int32 [8192], P(('sec', 'gx', 'gy')), may hold values from 0 to 7
- patch_weight: float32 [8192], P(('sec', 'gx', 'gy')), may hold values from 0.2 to 2
- rain: float32 [8192], P(('sec', 'gx', 'gy')), may hold values from 0.1 to 1
- root_decay: float32 [8], replicated, may hold values from 0.05 to 0.8
Outputs:
- residual: float32 [50, 128, 512], P(None, ('sec', 'gx'), 'gy')
- nitrate_out: float32 [10, 8192], P(None, ('sec', 'gx', 'gy'))
All inputs are finite; a program needn't handle non-finite values. No bound on the sum of `land_mask` on one device may be relied on, other than what follows from the above.
Results may differ from a plain program's by a relative error of at most 0.0003.
The roundings to bfloat16 on the way count: a program that leaves them out, or rounds other values in their place, can miss the bound.
Values may be sent and summed in bfloat16 or wider, within the bound.
No kernel may reach another device: no remote copies, remote signals or barrier semaphores. Data moves between devices by JAX's collectives and lax.ppermute only.
A program may use at most 192 MiB of HBM per device.

v0:
```python
import jax
import jax.numpy as jnp
from jax import lax
from jax.sharding import PartitionSpec as P

NSUB = 4


def with_halo(value, sides, width):
    for axis, dim in sides:
        peers, length = (lax.axis_size(axis), value.shape[dim])
        up = [(i, (i + 1) % peers) for i in range(peers - 1)]
        down = [(j, i) for i, j in up]
        last = lax.slice_in_dim(value, length - width, length, axis=dim)
        leading = lax.slice_in_dim(value, 0, width, axis=dim)
        before = lax.ppermute(last, axis, up)
        after = lax.ppermute(leading, axis, down)
        value = jnp.concatenate([before, value, after], axis=dim)
    return value


def saturation(head, alpha_field):
    suction = jax.nn.softplus(-head)
    scaled = alpha_field * suction
    return 1.0 / jnp.sqrt(1.0 + scaled * scaled)


def outflow(pressure, conduct, head_pad, cond_pad):
    head_x = head_pad[:, :, 1:-1]
    cond_x = cond_pad[:, :, 1:-1]
    flux_x = 0.5 * (cond_x[:, :-1] + cond_x[:, 1:]) * (head_x[:, :-1] - head_x[:, 1:])
    head_y = head_pad[:, 1:-1, :]
    cond_y = cond_pad[:, 1:-1, :]
    flux_y = 0.5 * (cond_y[:, :, :-1] + cond_y[:, :, 1:]) * (head_y[:, :, :-1] - head_y[:, :, 1:])
    flux_z = 0.5 * (conduct[:-1] + conduct[1:]) * (pressure[:-1] - pressure[1:] + 1.0)
    zero_top = jnp.zeros_like(conduct[:1])
    flux_z = jnp.concatenate([zero_top, flux_z, conduct[-1:]], 0)
    return (
        flux_x[:, 1:]
        - flux_x[:, :-1]
        + (flux_y[:, :, 1:] - flux_y[:, :, :-1])
        + (flux_z[1:] - flux_z[:-1])
    )


def deposit(values, targets, columns):
    slots = targets.shape[0]
    stride = 512 if slots % 512 == 0 else slots
    cells = jnp.arange(columns, dtype=jnp.int32)
    total = jnp.zeros((values.shape[0], columns), jnp.float32)
    for start in range(0, slots, stride):
        onehot = (targets[start : start + stride, None] == cells[None, :]).astype(jnp.float32)
        total = total + jnp.dot(
            values[:, start : start + stride],
            onehot,
            precision=lax.Precision.HIGHEST,
            preferred_element_type=jnp.float32,
        )
    return total


def patch_sources(sat_p, kinds_of, root_decay, weights, rainfall, top):
    kinds = jnp.arange(root_decay.shape[0], dtype=jnp.int32)
    decay = jnp.sum(
        jnp.where(kinds_of[None, :] == kinds[:, None], root_decay[:, None], 0.0), axis=0
    )
    levels = jnp.arange(top, dtype=jnp.float32) + 0.5
    profile = jnp.exp(-levels[:, None] * decay[None, :])
    profile = profile / jnp.sum(profile, axis=0, keepdims=True)
    extraction = weights[None, :] * profile * sat_p
    inflow = rainfall * (1.0 - sat_p[0])
    return jnp.concatenate([(inflow - extraction[0])[None], -extraction[1:]], 0)


def per_device(
    pressure,
    pressure_old,
    conductivity,
    vg_alpha,
    porosity,
    land_mask,
    nitrate,
    patch_column,
    crop_type,
    patch_weight,
    rain,
    root_decay,
):
    layers, width_x, width_y = pressure.shape
    top = nitrate.shape[0]
    kind_count = root_decay.shape[0]
    columns = width_x * width_y
    slots = patch_column.shape[0]
    owners = lax.axis_size(("gx", "gy"))
    per_block = slots // owners
    wet = saturation(pressure, vg_alpha)
    wet_old = saturation(pressure_old, vg_alpha)
    conduct = conductivity * wet * wet * wet
    sat_top = wet[:top].reshape(top, columns).astype(jnp.bfloat16)
    coded = patch_column * kind_count + crop_type
    codes_in = lax.all_to_all(
        coded.reshape(1, slots), ("gx", "gy"), split_axis=1, concat_axis=1, tiled=True
    )[0]
    ids_in = codes_in // kind_count
    whole = lax.all_gather(sat_top, ("gx", "gy"), axis=1, tiled=True)
    offsets = jnp.arange(slots, dtype=jnp.int32) // per_block * columns
    patch_sat = jnp.take(whole, offsets + patch_column, axis=1)
    sat_p = patch_sat.astype(jnp.float32)
    sources = patch_sources(sat_p, crop_type, root_decay, patch_weight, rain, top)
    received = lax.all_to_all(
        sources.astype(jnp.bfloat16), ("gx", "gy"), split_axis=1, concat_axis=1, tiled=True
    ).astype(sources.dtype)
    nitrogen = nitrate
    for step in range(NSUB):
        upper = jnp.concatenate([nitrogen[:1], nitrogen[:-1]], 0)
        lower = jnp.concatenate([nitrogen[1:], nitrogen[-1:]], 0)
        nitrogen = (
            nitrogen + 0.2 * (upper + lower - 2.0 * nitrogen) - 0.3 * sat_p * sat_p * nitrogen
        )
    stacked = jnp.stack([pressure, conduct])
    padded = with_halo(stacked, ((("sec", "gx"), 2), ("gy", 3)), 1)
    residual = porosity * (wet - wet_old) + outflow(pressure, conduct, padded[0], padded[1])
    column_source = deposit(received, ids_in, columns).reshape(top, width_x, width_y)
    column_source = column_source * land_mask.astype(jnp.float32)[None]
    residual = jnp.concatenate([residual[:top] - column_source, residual[top:]], 0)
    return (residual, nitrogen)


def solution(mesh):
    placed = (
        P(None, ("sec", "gx"), "gy"),
        P(None, ("sec", "gx"), "gy"),
        P(None, ("sec", "gx"), "gy"),
        P(None, ("sec", "gx"), "gy"),
        P(None, ("sec", "gx"), "gy"),
        P(("sec", "gx"), "gy"),
        P(None, ("sec", "gx", "gy")),
        P(("sec", "gx", "gy")),
        P(("sec", "gx", "gy")),
        P(("sec", "gx", "gy")),
        P(("sec", "gx", "gy")),
        P(),
    )
    return jax.shard_map(
        per_device,
        mesh=mesh,
        in_specs=placed,
        out_specs=(P(None, ("sec", "gx"), "gy"), P(None, ("sec", "gx", "gy"))),
        check_vma=False,
    )
```

profile of v0, /device:TPU:0, one launch (start us, length us, event | category | flops | bytes accessed | tf_op | source)
XLA Modules:
  0.0 239.4 jit_solution(622747574008032368)
XLA Ops:
  0.7 1.8 multiply_multiply_fusion
  2.5 1.3 collective-permute-start.1
  3.8 3.0 %collective-permute-start = (f32[2,50,1,128]{3,1,2,0:T(8,128)S(1)}, f32[2,50,1,128]{3,1,2,0:T(8,128)S(1)}, u32[]{:S(2)}, u32[]{:S(2)}) collective-permute-start(f32[2,50,1,128]{3,1,2,0:T(8,128)S(1)} %get-tuple-element.22), channel_id=1, source_target_pairs={{0,4},{4,8},{8,12},{12,16},{16,20},{20,24},{24,28},{1,5},{5,9},{9,... | collective-permute-start | bytes 153608 | tf_op jit(solution)/shard_map/ppermute | solution.py:16
  6.9 0.7 all_to_all.14
  7.6 9.0 %all-to-all-start.1 = ((s32[1,16,16]{2,0,1:T(1,128)}), s32[1,16,16]{2,0,1:T(1,128)S(1)}, u32[]{:S(2)}, u32[]{:S(2)}) async-start(s32[1,16,16]{2,0,1:T(1,128)} %all_to_all.14), calls=%async_computation.1 | async-start | bytes 16384 | tf_op jit(solution)/shard_map/all_to_all | solution.py:101
  16.6 0.3 copy.207
  16.9 0.0 copy-start.16
  16.9 190.1 %all_gather.3 = bf16[10,32768]{0,1:T(8,128)(2,1)} all-gather(bf16[10,2048]{0,1:T(8,128)(2,1)S(1)} %bitcast.27), channel_id=1, replica_groups=mesh['sec'=2,'gx'=4,'gy'=4] {'gx','gy'}, dimensions={1}, use_global_device_ids=true | all-gather | bytes 696320 | tf_op jit(solution)/shard_map/all_gather | solution.py:105
  207.0 5.2 %gather_fusion = bf16[256,10]{1,0:T(8,128)(2,1)S(1)} fusion(bf16[10,32768]{0,1:T(8,128)(2,1)} %all_gather.3, s32[1024]{0:T(1024)S(1)} %pad_clamp_fusion), kind=kCustom, calls=%fused_computation | custom fusion | bytes 11264 | tf_op jit(solution)/shard_map/jit(_take)/gather | solution.py:107
  212.2 0.1 copy.202
  212.5 0.1 select_reduce_fusion
  212.6 0.1 fusion.47
  212.7 0.6 fusion.46
  213.4 0.9 fusion.26
  214.3 0.1 concatenate.54
  214.4 0.1 concatenate.65
  214.5 0.7 pad_maximum_fusion.3
  215.2 0.6 multiply_add_fusion
  215.8 0.6 slice.219
  216.4 0.6 convert_element_type.16
  217.0 3.5 %all-to-all-start = ((bf16[10,16,16]{2,0,1:T(8,128)(2,1)}), bf16[10,16,16]{2,0,1:T(8,128)(2,1)S(1)}, u32[]{:S(2)}, u32[]{:S(2)}) async-start(bf16[10,16,16]{2,0,1:T(8,128)(2,1)} %pad_maximum_fusion.3), calls=%async_computation | async-start | bytes 131072 | tf_op jit(solution)/shard_map/all_to_all | solution.py:110
  220.5 0.5 broadcast.146
  221.0 0.6 reduce.3
  221.6 0.1 squeeze.16
  221.7 0.6 copy-done.4
  222.3 0.6 copy-done.6
  222.9 0.1 pad_maximum_fusion.1
  223.0 0.3 fusion.51
  223.3 1.0 copy.195
  224.4 1.3 collective-permute-start.3
  225.6 0.4 copy.194
  226.1 5.1 %collective-permute-start.2 = (f32[2,50,18,1]{1,0,3,2:T(2,128)S(1)}, f32[2,50,18,1]{1,0,3,2:T(2,128)}, u32[]{:S(2)}, u32[]{:S(2)}) collective-permute-start(f32[2,50,18,1]{1,0,3,2:T(2,128)S(1)} %copy.194), channel_id=1, source_target_pairs={{0,1},{1,2},{2,3},{4,5},{5,6},{6,7},{8,9},{9,10},{10,11},{12,13},{... | collective-permute-start | bytes 21608 | tf_op jit(solution)/shard_map/ppermute | solution.py:16
  231.2 0.6 and_select_fusion
  231.9 0.7 reshape.92
  232.6 0.5 copy.197
  233.0 1.2 copy.196
  234.3 0.9 pad_maximum_fusion
  235.1 0.2 slice_bitcast_fusion.1
  235.3 0.5 fusion.10
  235.8 0.0 copy-start.1
  235.9 0.6 fusion.12
  236.5 0.4 copy-done
  236.9 0.1 copy-done.1
  237.0 0.1 copy-done.2
  237.1 0.1 copy-done.3
  237.3 0.7 fusion.24
  238.1 0.5 fusion.5
  238.6 0.8 copy.206
  (64 shorter events, 0.4 us)
Async XLA Ops:
  0.6 6.2 %copy-start.14 = (s32[256]{0:T(256)S(1)}, s32[256]{0:T(256)}, u32[]{:S(2)}) copy-start(s32[256]{0:T(256)} %param.19) | copy-start | bytes 3076
  0.6 6.2 %copy-start.15 = (s32[256]{0:T(256)S(1)}, s32[256]{0:T(256)}, u32[]{:S(2)}) copy-start(s32[256]{0:T(256)} %param.20) | copy-start | bytes 3076
  0.7 15.9 %copy-start.8 = (f32[10,256]{1,0:T(8,128)S(1)}, f32[10,256]{1,0:T(8,128)}, u32[]{:S(2)}) copy-start(f32[10,256]{1,0:T(8,128)} %param.18) | copy-start | bytes 30724
  2.5 219.2 %collective-permute-start.1 = (f32[2,50,1,128]{3,1,2,0:T(8,128)S(1)}, f32[2,50,1,128]{3,1,2,0:T(8,128)S(1)}, u32[]{:S(2)}, u32[]{:S(2)}) collective-permute-start(f32[2,50,1,128]{3,1,2,0:T(8,128)S(1)} %get-tuple-element.23), channel_id=1, source_target_pairs={{4,0},{8,4},{12,8},{16,12},{20,16},{24,20},{28,24},{5,1},{9,5},{13... | collective-permute-start | bytes 153608 | tf_op jit(solution)/shard_map/ppermute | solution.py:17
  3.8 217.9 %collective-permute-start = (f32[2,50,1,128]{3,1,2,0:T(8,128)S(1)}, f32[2,50,1,128]{3,1,2,0:T(8,128)S(1)}, u32[]{:S(2)}, u32[]{:S(2)}) collective-permute-start(f32[2,50,1,128]{3,1,2,0:T(8,128)S(1)} %get-tuple-element.22), channel_id=1, source_target_pairs={{0,4},{4,8},{8,12},{12,16},{16,20},{20,24},{24,28},{1,5},{5,9},{9,... | collective-permute-start | bytes 153608 | tf_op jit(solution)/shard_map/ppermute | solution.py:16
  7.6 209.4 %all-to-all-start.1 = ((s32[1,16,16]{2,0,1:T(1,128)}), s32[1,16,16]{2,0,1:T(1,128)S(1)}, u32[]{:S(2)}, u32[]{:S(2)}) async-start(s32[1,16,16]{2,0,1:T(1,128)} %all_to_all.14), calls=%async_computation.1 | async-start | bytes 16384 | tf_op jit(solution)/shard_map/all_to_all | solution.py:101
  16.9 195.6 %copy-start.19 = (f32[8]{0:T(128)S(1)}, f32[8]{0:T(128)}, u32[]{:S(2)}) copy-start(f32[8]{0:T(128)} %param.23) | copy-start | bytes 100
  16.9 195.8 %copy-start.16 = (f32[256]{0:T(256)S(1)}, f32[256]{0:T(256)}, u32[]{:S(2)}) copy-start(f32[256]{0:T(256)} %param.21) | copy-start | bytes 3076
  207.0 7.4 %copy-start.17 = (f32[256]{0:T(256)S(1)}, f32[256]{0:T(256)}, u32[]{:S(2)}) copy-start(f32[256]{0:T(256)} %param.22) | copy-start | bytes 3076
  207.0 9.4 %copy-start.10 = (s32[16,128]{1,0:T(8,128)S(1)}, s32[16,128]{1,0:T(8,128)}, u32[]{:S(2)}) copy-start(s32[16,128]{1,0:T(8,128)} %param.17) | copy-start | bytes 24580
  217.0 14.8 %all-to-all-start = ((bf16[10,16,16]{2,0,1:T(8,128)(2,1)}), bf16[10,16,16]{2,0,1:T(8,128)(2,1)S(1)}, u32[]{:S(2)}, u32[]{:S(2)}) async-start(bf16[10,16,16]{2,0,1:T(8,128)(2,1)} %pad_maximum_fusion.3), calls=%async_computation | async-start | bytes 131072 | tf_op jit(solution)/shard_map/all_to_all | solution.py:110
  221.7 0.6 copy-start.4
  222.3 0.6 copy-start.6
  224.4 8.2 %collective-permute-start.3 = (f32[2,50,18,1]{1,0,3,2:T(2,128)}, f32[2,50,18,1]{1,0,3,2:T(2,128)S(1)}, u32[]{:S(2)}, u32[]{:S(2)}) collective-permute-start(f32[2,50,18,1]{1,0,3,2:T(2,128)} %copy.195), channel_id=1, source_target_pairs={{1,0},{2,1},{3,2},{5,4},{6,5},{7,6},{9,8},{10,9},{11,10},{13,12},{... | collective-permute-start | bytes 21608 | tf_op jit(solution)/shard_map/ppermute | solution.py:17
  226.1 7.0 %collective-permute-start.2 = (f32[2,50,18,1]{1,0,3,2:T(2,128)S(1)}, f32[2,50,18,1]{1,0,3,2:T(2,128)}, u32[]{:S(2)}, u32[]{:S(2)}) collective-permute-start(f32[2,50,18,1]{1,0,3,2:T(2,128)S(1)} %copy.194), channel_id=1, source_target_pairs={{0,1},{1,2},{2,3},{4,5},{5,6},{6,7},{8,9},{9,10},{10,11},{12,13},{... | collective-permute-start | bytes 21608 | tf_op jit(solution)/shard_map/ppermute | solution.py:16
  231.8 2.4 %copy-start.5 = (f32[2,50,1,128]{3,1,2,0:T(8,128)S(1)}, f32[2,50,1,128]{3,1,2,0:T(8,128)}, u32[]{:S(2)}) copy-start(f32[2,50,1,128]{3,1,2,0:T(8,128)} %copy-done.4) | copy-start | bytes 153604
  231.8 2.4 %copy-start.7 = (f32[2,50,1,128]{3,1,2,0:T(8,128)S(1)}, f32[2,50,1,128]{3,1,2,0:T(8,128)}, u32[]{:S(2)}) copy-start(f32[2,50,1,128]{3,1,2,0:T(8,128)} %copy-done.6) | copy-start | bytes 153604
  235.8 1.0 copy-start
  235.8 1.1 copy-start.1
  235.9 1.2 copy-start.2
  235.9 1.4 copy-start.3
  235.9 1.4 copy-start.9
  237.2 0.8 copy-start.11
  237.2 0.8 copy-start.12
  237.2 0.8 copy-start.13
  237.2 0.8 copy-start.18
where the time goes:
time: 240 us; the launch traced here: 239 us
  blocking collectives  190 us (79%)
  starting transfers between devices  23.2 us (10%)
  local copies, waits for them, and re-layouts  15 us (6%)
  other arithmetic  9.55 us (4%)
    all_gather x1, blocking collectives, per_device(): whole = lax.all_gather(sat_top, ('gx', 'gy'), axis=1, tiled=True)  190 us
    all_to_all x1, starting transfers between devices, per_device(): lax.all_to_all(coded.reshape(1, slots), ('gx', 'gy'), split_axis=1, conca...  8.96 us
    ppermute x2, starting transfers between devices, with_halo(): before = lax.ppermute(last, axis, up)  8.17 us
    gather x2, local copies, waits for them, and re-layouts, per_device(): patch_sat = jnp.take(whole, offsets + patch_column, axis=1)  5.29 us
  transfers between devices with their start and end apart: 6, of which 0 were waited for; matrix products, arithmetic and copies ran while one was open for 6% of the time, Pallas kernels for 0%

commit v1 on v0

--- a/solution.py
+++ b/solution.py
@@ -4,6 +4,12 @@
 from jax.sharding import PartitionSpec as P
 
 NSUB = 4
+
+
+def laid_out(blocks, dim):
+    dims = list(blocks.shape[1:])
+    dims[dim] *= blocks.shape[0]
+    return jnp.moveaxis(blocks, 0, dim).reshape(dims)
 
 
 def with_halo(value, sides, width):
@@ -102,7 +108,19 @@
         coded.reshape(1, slots), ("gx", "gy"), split_axis=1, concat_axis=1, tiled=True
     )[0]
     ids_in = codes_in // kind_count
-    whole = lax.all_gather(sat_top, ("gx", "gy"), axis=1, tiled=True)
+    length_2 = lax.axis_size(("gx", "gy"))
+    pairs = [(i_2, (i_2 + 1) % length_2) for i_2 in range(length_2)]
+    back = [(b, a) for a, b in pairs]
+    lower_2, upper_2 = ([], [])
+    for k in range(length_2 - 1):
+        if k % 2 == 0:
+            lower_2.append(lax.ppermute(lower_2[-1] if lower_2 else sat_top, ("gx", "gy"), pairs))
+        else:
+            upper_2.append(lax.ppermute(upper_2[-1] if upper_2 else sat_top, ("gx", "gy"), back))
+    blocks = jnp.stack([*lower_2[::-1], sat_top, *upper_2])
+    shift = lax.axis_index(("gx", "gy")) - len(lower_2)
+    blocks = blocks[(jnp.arange(length_2) - shift) % length_2]
+    whole = laid_out(blocks, 1)
     offsets = jnp.arange(slots, dtype=jnp.int32) // per_block * columns
     patch_sat = jnp.take(whole, offsets + patch_column, axis=1)
     sat_p = patch_sat.astype(jnp.float32)

time: 240 us -> 110 us (0.46)
  blocking collectives: 190 us -> 0 us
  starting transfers between devices: 23.2 us -> 51.9 us
  waiting for transfers between devices: 0.02 us -> 13.7 us
  other arithmetic: 9.55 us -> 18.4 us
  local copies, waits for them, and re-layouts: 15 us -> 23.5 us
    all_gather x1 -> x0, blocking collectives: 190 us -> none  [per_device(): whole = lax.all_gather(sat_top, ('gx', 'gy'), axis=1, tiled=True)]
    ppermute x0 -> x15, starting transfers between devices: none -> 32.6 us  [the longest x7 28 us: per_device(): lax.ppermute(upper_2[-1] if upper_2 else sat_top, ('gx', 'gy'), back)]
    ppermute x0 -> x15, waiting for transfers between devices: none -> 8.31 us  [the longest x8 5.07 us: per_device(): lax.ppermute(lower_2[-1] if lower_2 else sat_top, ('gx', 'gy'), pairs)]
    reshape x0 -> x1, local copies, waits for them, and re-layouts: none -> 6.17 us  [laid_out(): return jnp.moveaxis(blocks, 0, dim).reshape(dims)]
    all_to_all x1, waiting for transfers between devices: 0.01 us -> 4.88 us  [per_device(): lax.all_to_all(sources.astype(jnp.bfloat16), ('gx', 'gy'), split_axis=1,...]
    all_to_all x1, starting transfers between devices: 8.96 us -> 4.91 us  [per_device(): lax.all_to_all(coded.reshape(1, slots), ('gx', 'gy'), split_axis=1, conca...]
    sub x4, other arithmetic: 0.71 us -> 3.5 us  [per_device(): nitrogen + 0.2 * (upper + lower - 2.0 * nitrogen)]
  transfers between devices with their start and end apart: 6 -> 21, of which waited for: 0 -> 11; matrix products, arithmetic and copies ran while one was open for 6% -> 18% of each run, Pallas kernels for 0% -> 0%
where the time goes in v1:
time: 110 us; the launch traced here: 109 us
  starting transfers between devices  51.9 us (47%)
  local copies, waits for them, and re-layouts  23.5 us (21%)
  other arithmetic  18.4 us (17%)
  waiting for transfers between devices  13.7 us (12%)
  between operations  1.16 us (1%)
    ppermute x7, starting transfers between devices, per_device(): lax.ppermute(upper_2[-1] if upper_2 else sat_top, ('gx', 'gy'), back)  28 us
    ppermute x2, starting transfers between devices, with_halo(): before = lax.ppermute(last, axis, up)  8.18 us
    reshape x1, local copies, waits for them, and re-layouts, laid_out(): return jnp.moveaxis(blocks, 0, dim).reshape(dims)  6.17 us
    gather x2, local copies, waits for them, and re-layouts, per_device(): patch_sat = jnp.take(whole, offsets + patch_column, axis=1)  5.48 us
    ppermute x8, waiting for transfers between devices, per_device(): lax.ppermute(lower_2[-1] if lower_2 else sat_top, ('gx', 'gy'), pairs)  5.07 us
    all_to_all x1, starting transfers between devices, per_device(): lax.all_to_all(coded.reshape(1, slots), ('gx', 'gy'), split_axis=1, conca...  4.91 us
    all_to_all x1, waiting for transfers between devices, per_device(): lax.all_to_all(sources.astype(jnp.bfloat16), ('gx', 'gy'), split_axis=1,...  4.88 us
    ppermute x8, starting transfers between devices, per_device(): lax.ppermute(lower_2[-1] if lower_2 else sat_top, ('gx', 'gy'), pairs)  4.66 us
  transfers between devices with their start and end apart: 21, of which 11 were waited for; matrix products, arithmetic and copies ran while one was open for 18% of the time, Pallas kernels for 0%

profile of v1, /device:TPU:0, one launch (start us, length us, event | category | flops | bytes accessed | tf_op | source)
XLA Modules:
  0.0 109.1 jit_solution(5815506025183570456)
XLA Ops:
  0.7 1.6 %multiply_multiply_fusion = (f32[50,16,128]{2,1,0:T(8,128)S(1)}, f32[50,16,128]{2,1,0:T(8,128)S(1)}) fusion(f32[50,16,128]{2,1,0:T(8,128)} %param.14, f32[50,16,128]{2,1,0:T(8,128)} %param.15, f32[50,16,128]{2,1,0:T(8,128)} %param.12), kind=kLoop, calls=%fused_computation.20 | loop fusion | flops 1331200 | bytes 2048000 | tf_op jit(solution)/shard_map/mul | solution.py:104
  2.3 0.7 copy-done.1
  3.1 3.1 %collective-permute-start.4 = (bf16[10,2048]{1,0:T(8,128)(2,1)S(1)}, bf16[10,2048]{1,0:T(8,128)(2,1)S(1)}, u32[]{:S(2)}, u32[]{:S(2)}) collective-permute-start(bf16[10,2048]{1,0:T(8,128)(2,1)S(1)} %bitcast.68), channel_id=1, source_target_pairs={{0,1},{1,2},{2,3},{3,4},{4,5},{5,6},{6,7},{7,8},{8,9},{9,10},{10,1... | collective-permute-start | bytes 122888 | tf_op jit(solution)/shard_map/ppermute | solution.py:117
  6.2 2.5 %collective-permute-start.12 = (bf16[10,2048]{1,0:T(8,128)(2,1)S(1)}, bf16[10,2048]{1,0:T(8,128)(2,1)S(1)}, u32[]{:S(2)}, u32[]{:S(2)}) collective-permute-start(bf16[10,2048]{1,0:T(8,128)(2,1)S(1)} %bitcast.69), channel_id=1, source_target_pairs={{1,0},{2,1},{3,2},{4,3},{5,4},{6,5},{7,6},{8,7},{9,8},{10,9},{11,1... | collective-permute-start | bytes 122888 | tf_op jit(solution)/shard_map/ppermute | solution.py:119
  8.8 1.4 %collective-permute-start.1 = (f32[2,50,1,128]{3,2,1,0:T(1,128)S(1)}, f32[2,50,1,128]{3,2,1,0:T(1,128)S(1)}, u32[]{:S(2)}, u32[]{:S(2)}) collective-permute-start(f32[2,50,1,128]{3,2,1,0:T(1,128)S(1)} %get-tuple-element.23), channel_id=1, source_target_pairs={{4,0},{8,4},{12,8},{16,12},{20,16},{24,20},{28,24},{5,1},{9,5},{13... | collective-permute-start | bytes 153608 | tf_op jit(solution)/shard_map/ppermute | solution.py:23
  10.2 3.0 %collective-permute-start = (f32[2,50,1,128]{3,2,1,0:T(1,128)S(1)}, f32[2,50,1,128]{3,2,1,0:T(1,128)S(1)}, u32[]{:S(2)}, u32[]{:S(2)}) collective-permute-start(f32[2,50,1,128]{3,2,1,0:T(1,128)S(1)} %get-tuple-element.22), channel_id=1, source_target_pairs={{0,4},{4,8},{8,12},{12,16},{16,20},{20,24},{24,28},{1,5},{5,9},{9,... | collective-permute-start | bytes 153608 | tf_op jit(solution)/shard_map/ppermute | solution.py:22
  13.3 0.7 all_to_all.14
  14.0 4.9 %all-to-all-start.1 = ((s32[1,16,16]{2,0,1:T(1,128)}), s32[1,16,16]{2,0,1:T(1,128)S(1)}, u32[]{:S(2)}, u32[]{:S(2)}) async-start(s32[1,16,16]{2,0,1:T(1,128)} %all_to_all.14), calls=%async_computation.1 | async-start | bytes 16384 | tf_op jit(solution)/shard_map/all_to_all | solution.py:107
  18.9 0.9 fusion.22
  22.9 0.7 fusion.40
  25.8 0.7 reduce.3
  26.6 1.5 %collective-permute-start.5 = (bf16[10,2048]{1,0:T(8,128)(2,1)S(1)}, bf16[10,2048]{1,0:T(8,128)(2,1)}, u32[]{:S(2)}, u32[]{:S(2)}) collective-permute-start(bf16[10,2048]{1,0:T(8,128)(2,1)S(1)} %collective-permute-done.4), channel_id=1, source_target_pairs={{0,1},{1,2},{2,3},{3,4},{4,5},{5,6},{6,7},{7,8},{8,9},{9,10},{10,1... | collective-permute-start | bytes 122888 | tf_op jit(solution)/shard_map/ppermute | solution.py:117
  28.1 3.0 %collective-permute-start.13 = (bf16[10,2048]{1,0:T(8,128)(2,1)S(1)}, bf16[10,2048]{1,0:T(8,128)(2,1)}, u32[]{:S(2)}, u32[]{:S(2)}) collective-permute-start(bf16[10,2048]{1,0:T(8,128)(2,1)S(1)} %collective-permute-done.12), channel_id=1, source_target_pairs={{1,0},{2,1},{3,2},{4,3},{5,4},{6,5},{7,6},{8,7},{9,8},{10,9},{11,1... | collective-permute-start | bytes 122888 | tf_op jit(solution)/shard_map/ppermute | solution.py:119
  31.3 2.3 %collective-permute-done.5 = bf16[10,2048]{1,0:T(8,128)(2,1)} collective-permute-done((bf16[10,2048]{1,0:T(8,128)(2,1)S(1)}, bf16[10,2048]{1,0:T(8,128)(2,1)}, u32[]{:S(2)}, u32[]{:S(2)}) %collective-permute-start.5) | collective-permute-done | bytes 40992 | tf_op jit(solution)/shard_map/ppermute | solution.py:117
  34.1 1.0 copy.218
  35.1 1.3 %collective-permute-start.3 = (f32[2,50,18,1]{1,0,3,2:T(2,128)}, f32[2,50,18,1]{1,0,3,2:T(2,128)S(1)}, u32[]{:S(2)}, u32[]{:S(2)}) collective-permute-start(f32[2,50,18,1]{1,0,3,2:T(2,128)} %copy.218), channel_id=1, source_target_pairs={{1,0},{2,1},{3,2},{5,4},{6,5},{7,6},{9,8},{10,9},{11,10},{13,12},{... | collective-permute-start | bytes 21608 | tf_op jit(solution)/shard_map/ppermute | solution.py:23
  36.9 5.1 %collective-permute-start.2 = (f32[2,50,18,1]{1,0,3,2:T(2,128)S(1)}, f32[2,50,18,1]{1,0,3,2:T(2,128)}, u32[]{:S(2)}, u32[]{:S(2)}) collective-permute-start(f32[2,50,18,1]{1,0,3,2:T(2,128)S(1)} %copy.217), channel_id=1, source_target_pairs={{0,1},{1,2},{2,3},{4,5},{5,6},{6,7},{8,9},{9,10},{10,11},{12,13},{... | collective-permute-start | bytes 21608 | tf_op jit(solution)/shard_map/ppermute | solution.py:22
  43.2 1.3 %copy.219 = f32[2,50,18,1]{3,2,1,0:T(8,128)S(1)} copy(f32[2,50,18,1]{1,0,3,2:T(2,128)} %collective-permute-done.2) | data formatting | bytes 14400 | tf_op jit(solution)/shard_map/ppermute | solution.py:22
  44.5 4.5 %collective-permute-start.14 = (bf16[10,2048]{1,0:T(8,128)(2,1)}, bf16[10,2048]{1,0:T(8,128)(2,1)S(1)}, u32[]{:S(2)}, u32[]{:S(2)}) collective-permute-start(bf16[10,2048]{1,0:T(8,128)(2,1)} %collective-permute-done.13), channel_id=1, source_target_pairs={{1,0},{2,1},{3,2},{4,3},{5,4},{6,5},{7,6},{8,7},{9,8},{10,9},{11,1... | collective-permute-start | bytes 122888 | tf_op jit(solution)/shard_map/ppermute | solution.py:119
  49.0 1.5 %pad_maximum_fusion = f32[2,50,18,130]{3,2,1,0:T(8,128)S(1)} fusion(f32[2,50,18,1]{3,2,1,0:T(8,128)S(1)} %copy.220, f32[2,50,1,128]{3,2,1,0:T(1,128)S(1)} %collective-permute-done.1, f32[1,50,16,128]{3,2,1,0:T(8,128)S(1)} %bitcast.61, f32[1,50,16,128]{3,2,1,0:T(8,128)S(1)} %bitcast.64, f32[2,50,1,128]{3,2,1,0:T(1,128)S(1)} %collective-permute-done, ...), kind=kLoop, calls=%fused_computation.2 | loop fusion | flops 1170000 | bytes 1872000 | tf_op jit(solution)/shard_map/concatenate | solution.py:24
  50.4 0.7 collective-permute-done.14
  51.2 4.4 %collective-permute-start.15 = (bf16[10,2048]{1,0:T(8,128)(2,1)S(1)}, bf16[10,2048]{1,0:T(8,128)(2,1)S(1)}, u32[]{:S(2)}, u32[]{:S(2)}) collective-permute-start(bf16[10,2048]{1,0:T(8,128)(2,1)S(1)} %collective-permute-done.14), channel_id=1, source_target_pairs={{1,0},{2,1},{3,2},{4,3},{5,4},{6,5},{7,6},{8,7},{9,8},{10,9},{11,1... | collective-permute-start | bytes 122888 | tf_op jit(solution)/shard_map/ppermute | solution.py:119
  55.9 1.6 %collective-permute-done.15 = bf16[10,2048]{1,0:T(8,128)(2,1)S(1)} collective-permute-done((bf16[10,2048]{1,0:T(8,128)(2,1)S(1)}, bf16[10,2048]{1,0:T(8,128)(2,1)S(1)}, u32[]{:S(2)}, u32[]{:S(2)}) %collective-permute-start.15) | collective-permute-done | bytes 40992 | tf_op jit(solution)/shard_map/ppermute | solution.py:119
  57.5 4.5 %collective-permute-start.16 = (bf16[10,2048]{1,0:T(8,128)(2,1)S(1)}, bf16[10,2048]{1,0:T(8,128)(2,1)S(1)}, u32[]{:S(2)}, u32[]{:S(2)}) collective-permute-start(bf16[10,2048]{1,0:T(8,128)(2,1)S(1)} %collective-permute-done.15), channel_id=1, source_target_pairs={{1,0},{2,1},{3,2},{4,3},{5,4},{6,5},{7,6},{8,7},{9,8},{10,9},{11,1... | collective-permute-start | bytes 122888 | tf_op jit(solution)/shard_map/ppermute | solution.py:119
  62.0 0.8 collective-permute-done.9
  63.9 4.5 %collective-permute-start.17 = (bf16[10,2048]{1,0:T(8,128)(2,1)S(1)}, bf16[10,2048]{1,0:T(8,128)(2,1)S(1)}, u32[]{:S(2)}, u32[]{:S(2)}) collective-permute-start(bf16[10,2048]{1,0:T(8,128)(2,1)S(1)} %collective-permute-done.16), channel_id=1, source_target_pairs={{1,0},{2,1},{3,2},{4,3},{5,4},{6,5},{7,6},{8,7},{9,8},{10,9},{11,1... | collective-permute-start | bytes 122888 | tf_op jit(solution)/shard_map/ppermute | solution.py:119
  68.4 0.9 collective-permute-done.10
  69.3 0.7 fusion.6
  70.3 4.6 %collective-permute-start.18 = (bf16[10,2048]{1,0:T(8,128)(2,1)S(1)}, bf16[10,2048]{1,0:T(8,128)(2,1)S(1)}, u32[]{:S(2)}, u32[]{:S(2)}) collective-permute-start(bf16[10,2048]{1,0:T(8,128)(2,1)S(1)} %collective-permute-done.17), channel_id=1, source_target_pairs={{1,0},{2,1},{3,2},{4,3},{5,4},{6,5},{7,6},{8,7},{9,8},{10,9},{11,1... | collective-permute-start | bytes 122888 | tf_op jit(solution)/shard_map/ppermute | solution.py:119
  74.9 0.9 collective-permute-done.11
  75.8 0.8 bitcast_dynamic-update-slice_fusion.10
  76.7 0.8 bitcast_dynamic-update-slice_fusion.9
  77.5 0.8 bitcast_dynamic-update-slice_fusion.8
  78.4 0.8 bitcast_dynamic-update-slice_fusion.5
  79.3 0.7 gather_fusion
  80.1 6.2 %copy.228 = bf16[10,16,2048]{0,2,1:T(8,128)(2,1)} copy(bf16[10,16,2048]{2,0,1:T(8,128)(2,1)S(1)} %bitcast.66) | data formatting | bytes 1310720 | tf_op jit(solution)/shard_map/reshape | solution.py:12
  86.2 5.4 %gather_fusion.1 = bf16[256,10]{1,0:T(8,128)(2,1)S(1)} fusion(bf16[10,32768]{0,1:T(8,128)(2,1)} %bitcast.65, s32[1024]{0:T(1024)} %pad_clamp_fusion), kind=kCustom, calls=%fused_computation.1 | custom fusion | bytes 11264 | tf_op jit(solution)/shard_map/jit(_take)/gather | solution.py:125
  91.7 0.8 fusion.27
  92.5 0.7 fusion.31
  93.3 0.7 fusion.35
  94.0 1.3 %fusion.39 = (f32[10,256]{1,0:T(8,128)}, f32[10,256]{1,0:T(8,128)S(1)}) fusion(f32[10,256]{1,0:T(8,128)S(1)} %fusion.35, f32[9,256]{1,0:T(8,128)S(1)} %get-tuple-element.25, f32[1,256]{1,0:T(1,128)S(1)} %get-tuple-element.27, f32[1,256]{1,0:T(1,128)S(1)} %get-tuple-element.26, f32[9,256]{1,0:T(8,128)S(1)} %get-tuple-element.24, ...), kind=kLoop, calls=%fused_computation.85 | loop fusion | flops 43520 | bytes 59688 | tf_op jit(solution)/shard_map/sub | solution.py:136
  95.3 0.7 convert_bitcast_fusion
  96.1 0.7 subtract_convert_fusion
  96.9 0.7 pad_maximum_fusion.3
  97.6 3.5 %all-to-all-start = ((bf16[10,16,16]{2,0,1:T(8,128)(2,1)}), bf16[10,16,16]{2,0,1:T(8,128)(2,1)S(1)}, u32[]{:S(2)}, u32[]{:S(2)}) async-start(bf16[10,16,16]{2,0,1:T(8,128)(2,1)} %pad_maximum_fusion.3), calls=%async_computation | async-start | bytes 131072 | tf_op jit(solution)/shard_map/all_to_all | solution.py:128
  101.1 1.6 %fusion.18 = f32[50,16,128]{2,1,0:T(8,128)S(1)} fusion(f32[50,16,128]{2,1,0:T(8,128)} %param.16, f32[50,16,128]{2,1,0:T(8,128)S(1)} %copy-done.2, f32[50,16,128]{2,1,0:T(8,128)S(1)} %copy-done.3, f32[50,16,129]{2,1,0:T(8,128)S(1)} %fusion.4, f32[50,17,128]{2,1,0:T(8,128)S(1)} %fusion.6, f32[1,16,128]{2,1,0:T(8,128)S(1)} %slice.218, ...), kind=kLoop, calls=%fused_computation.31 | loop fusion | flops 1945600 | bytes 4096000 | tf_op jit(solution)/shard_map/add | solution.py:140
  102.8 4.9 %all-to-all-done = bf16[10,16,16]{2,0,1:T(8,128)(2,1)S(1)} async-done(((bf16[10,16,16]{2,0,1:T(8,128)(2,1)}), bf16[10,16,16]{2,0,1:T(8,128)(2,1)S(1)}, u32[]{:S(2)}, u32[]{:S(2)}) %all-to-all-start) | async-done | bytes 5152 | tf_op jit(solution)/shard_map/all_to_all | solution.py:128
  108.3 0.8 pad_maximum_fusion.2
  (109 shorter events, 10.7 us)
Async XLA Ops:
  0.6 8.0 %copy-start = (f32[50,16,128]{2,1,0:T(8,128)S(1)}, f32[50,16,128]{2,1,0:T(8,128)}, u32[]{:S(2)}) copy-start(f32[50,16,128]{2,1,0:T(8,128)} %param.12) | copy-start | bytes 1228804
  0.6 12.6 %copy-start.12 = (s32[256]{0:T(256)S(1)}, s32[256]{0:T(256)}, u32[]{:S(2)}) copy-start(s32[256]{0:T(256)} %param.19) | copy-start | bytes 3076
  0.7 12.6 %copy-start.13 = (s32[256]{0:T(256)S(1)}, s32[256]{0:T(256)}, u32[]{:S(2)}) copy-start(s32[256]{0:T(256)} %param.20) | copy-start | bytes 3076
  2.3 0.8 copy-start.1
  3.1 23.5 %collective-permute-start.4 = (bf16[10,2048]{1,0:T(8,128)(2,1)S(1)}, bf16[10,2048]{1,0:T(8,128)(2,1)S(1)}, u32[]{:S(2)}, u32[]{:S(2)}) collective-permute-start(bf16[10,2048]{1,0:T(8,128)(2,1)S(1)} %bitcast.68), channel_id=1, source_target_pairs={{0,1},{1,2},{2,3},{3,4},{4,5},{5,6},{6,7},{7,8},{8,9},{9,10},{10,1... | collective-permute-start | bytes 122888 | tf_op jit(solution)/shard_map/ppermute | solution.py:117
  6.2 21.9 %collective-permute-start.12 = (bf16[10,2048]{1,0:T(8,128)(2,1)S(1)}, bf16[10,2048]{1,0:T(8,128)(2,1)S(1)}, u32[]{:S(2)}, u32[]{:S(2)}) collective-permute-start(bf16[10,2048]{1,0:T(8,128)(2,1)S(1)} %bitcast.69), channel_id=1, source_target_pairs={{1,0},{2,1},{3,2},{4,3},{5,4},{6,5},{7,6},{8,7},{9,8},{10,9},{11,1... | collective-permute-start | bytes 122888 | tf_op jit(solution)/shard_map/ppermute | solution.py:119
  8.8 11.0 %copy-start.5 = (f32[10,256]{1,0:T(8,128)S(1)}, f32[10,256]{1,0:T(8,128)}, u32[]{:S(2)}) copy-start(f32[10,256]{1,0:T(8,128)} %param.18) | copy-start | bytes 30724
  8.8 14.0 %copy-start.16 = (f32[8]{0:T(128)S(1)}, f32[8]{0:T(128)}, u32[]{:S(2)}) copy-start(f32[8]{0:T(128)} %param.23) | copy-start | bytes 100
  8.8 15.4 %copy-start.9 = (s32[16,128]{1,0:T(8,128)S(1)}, s32[16,128]{1,0:T(8,128)}, u32[]{:S(2)}) copy-start(s32[16,128]{1,0:T(8,128)} %param.17) | copy-start | bytes 24580
  8.8 22.3 %collective-permute-start.1 = (f32[2,50,1,128]{3,2,1,0:T(1,128)S(1)}, f32[2,50,1,128]{3,2,1,0:T(1,128)S(1)}, u32[]{:S(2)}, u32[]{:S(2)}) collective-permute-start(f32[2,50,1,128]{3,2,1,0:T(1,128)S(1)} %get-tuple-element.23), channel_id=1, source_target_pairs={{4,0},{8,4},{12,8},{16,12},{20,16},{24,20},{28,24},{5,1},{9,5},{13... | collective-permute-start | bytes 153608 | tf_op jit(solution)/shard_map/ppermute | solution.py:23
  10.2 20.9 %collective-permute-start = (f32[2,50,1,128]{3,2,1,0:T(1,128)S(1)}, f32[2,50,1,128]{3,2,1,0:T(1,128)S(1)}, u32[]{:S(2)}, u32[]{:S(2)}) collective-permute-start(f32[2,50,1,128]{3,2,1,0:T(1,128)S(1)} %get-tuple-element.22), channel_id=1, source_target_pairs={{0,4},{4,8},{8,12},{12,16},{16,20},{20,24},{24,28},{1,5},{5,9},{9,... | collective-permute-start | bytes 153608 | tf_op jit(solution)/shard_map/ppermute | solution.py:22
  14.0 11.3 %all-to-all-start.1 = ((s32[1,16,16]{2,0,1:T(1,128)}), s32[1,16,16]{2,0,1:T(1,128)S(1)}, u32[]{:S(2)}, u32[]{:S(2)}) async-start(s32[1,16,16]{2,0,1:T(1,128)} %all_to_all.14), calls=%async_computation.1 | async-start | bytes 16384 | tf_op jit(solution)/shard_map/all_to_all | solution.py:107
  21.6 12.1 %copy-start.15 = (f32[10]{0:T(128)}, f32[10]{0:T(128)S(1)}, u32[]{:S(2)}) copy-start(f32[10]{0:T(128)S(1)} %add_negate_fusion) | copy-start | bytes 124
  22.9 10.8 %copy-start.11 = (f32[256]{0:T(256)}, f32[256]{0:T(256)S(1)}, u32[]{:S(2)}) copy-start(f32[256]{0:T(256)S(1)} %select_reduce_fusion) | copy-start | bytes 3076
  26.6 7.1 %copy-start.6 = (bf16[10,2048]{1,0:T(8,128)(2,1)}, bf16[10,2048]{1,0:T(8,128)(2,1)S(1)}, u32[]{:S(2)}) copy-start(bf16[10,2048]{1,0:T(8,128)(2,1)S(1)} %collective-permute-done.4) | copy-start | bytes 122884
  26.6 7.1 %collective-permute-start.5 = (bf16[10,2048]{1,0:T(8,128)(2,1)S(1)}, bf16[10,2048]{1,0:T(8,128)(2,1)}, u32[]{:S(2)}, u32[]{:S(2)}) collective-permute-start(bf16[10,2048]{1,0:T(8,128)(2,1)S(1)} %collective-permute-done.4), channel_id=1, source_target_pairs={{0,1},{1,2},{2,3},{3,4},{4,5},{5,6},{6,7},{7,8},{8,9},{9,10},{10,1... | collective-permute-start | bytes 122888 | tf_op jit(solution)/shard_map/ppermute | solution.py:117
  28.1 16.4 %collective-permute-start.13 = (bf16[10,2048]{1,0:T(8,128)(2,1)S(1)}, bf16[10,2048]{1,0:T(8,128)(2,1)}, u32[]{:S(2)}, u32[]{:S(2)}) collective-permute-start(bf16[10,2048]{1,0:T(8,128)(2,1)S(1)} %collective-permute-done.12), channel_id=1, source_target_pairs={{1,0},{2,1},{3,2},{4,3},{5,4},{6,5},{7,6},{8,7},{9,8},{10,9},{11,1... | collective-permute-start | bytes 122888 | tf_op jit(solution)/shard_map/ppermute | solution.py:119
  33.6 8.4 %collective-permute-start.6 = (bf16[10,2048]{1,0:T(8,128)(2,1)}, bf16[10,2048]{1,0:T(8,128)(2,1)}, u32[]{:S(2)}, u32[]{:S(2)}) collective-permute-start(bf16[10,2048]{1,0:T(8,128)(2,1)} %collective-permute-done.5), channel_id=1, source_target_pairs={{0,1},{1,2},{2,3},{3,4},{4,5},{5,6},{6,7},{7,8},{8,9},{9,10},{10,1... | collective-permute-start | bytes 122888 | tf_op jit(solution)/shard_map/ppermute | solution.py:117
  35.1 7.5 %collective-permute-start.3 = (f32[2,50,18,1]{1,0,3,2:T(2,128)}, f32[2,50,18,1]{1,0,3,2:T(2,128)S(1)}, u32[]{:S(2)}, u32[]{:S(2)}) collective-permute-start(f32[2,50,18,1]{1,0,3,2:T(2,128)} %copy.218), channel_id=1, source_target_pairs={{1,0},{2,1},{3,2},{5,4},{6,5},{7,6},{9,8},{10,9},{11,10},{13,12},{... | collective-permute-start | bytes 21608 | tf_op jit(solution)/shard_map/ppermute | solution.py:23
  36.9 6.3 %collective-permute-start.2 = (f32[2,50,18,1]{1,0,3,2:T(2,128)S(1)}, f32[2,50,18,1]{1,0,3,2:T(2,128)}, u32[]{:S(2)}, u32[]{:S(2)}) collective-permute-start(f32[2,50,18,1]{1,0,3,2:T(2,128)S(1)} %copy.217), channel_id=1, source_target_pairs={{0,1},{1,2},{2,3},{4,5},{5,6},{6,7},{8,9},{9,10},{10,11},{12,13},{... | collective-permute-start | bytes 21608 | tf_op jit(solution)/shard_map/ppermute | solution.py:22
  42.0 6.9 %collective-permute-start.7 = (bf16[10,2048]{1,0:T(8,128)(2,1)}, bf16[10,2048]{1,0:T(8,128)(2,1)}, u32[]{:S(2)}, u32[]{:S(2)}) collective-permute-start(bf16[10,2048]{1,0:T(8,128)(2,1)} %collective-permute-done.6), channel_id=1, source_target_pairs={{0,1},{1,2},{2,3},{3,4},{4,5},{5,6},{6,7},{7,8},{8,9},{9,10},{10,1... | collective-permute-start | bytes 122888 | tf_op jit(solution)/shard_map/ppermute | solution.py:117
  44.5 6.7 %collective-permute-start.14 = (bf16[10,2048]{1,0:T(8,128)(2,1)}, bf16[10,2048]{1,0:T(8,128)(2,1)S(1)}, u32[]{:S(2)}, u32[]{:S(2)}) collective-permute-start(bf16[10,2048]{1,0:T(8,128)(2,1)} %collective-permute-done.13), channel_id=1, source_target_pairs={{1,0},{2,1},{3,2},{4,3},{5,4},{6,5},{7,6},{8,7},{9,8},{10,9},{11,1... | collective-permute-start | bytes 122888 | tf_op jit(solution)/shard_map/ppermute | solution.py:119
  49.0 6.7 %collective-permute-start.8 = (bf16[10,2048]{1,0:T(8,128)(2,1)}, bf16[10,2048]{1,0:T(8,128)(2,1)S(1)}, u32[]{:S(2)}, u32[]{:S(2)}) collective-permute-start(bf16[10,2048]{1,0:T(8,128)(2,1)} %collective-permute-done.7), channel_id=1, source_target_pairs={{0,1},{1,2},{2,3},{3,4},{4,5},{5,6},{6,7},{7,8},{8,9},{9,10},{10,1... | collective-permute-start | bytes 122888 | tf_op jit(solution)/shard_map/ppermute | solution.py:117
  51.2 6.3 %collective-permute-start.15 = (bf16[10,2048]{1,0:T(8,128)(2,1)S(1)}, bf16[10,2048]{1,0:T(8,128)(2,1)S(1)}, u32[]{:S(2)}, u32[]{:S(2)}) collective-permute-start(bf16[10,2048]{1,0:T(8,128)(2,1)S(1)} %collective-permute-done.14), channel_id=1, source_target_pairs={{1,0},{2,1},{3,2},{4,3},{5,4},{6,5},{7,6},{8,7},{9,8},{10,9},{11,1... | collective-permute-start | bytes 122888 | tf_op jit(solution)/shard_map/ppermute | solution.py:119
  55.7 7.1 %collective-permute-start.9 = (bf16[10,2048]{1,0:T(8,128)(2,1)S(1)}, bf16[10,2048]{1,0:T(8,128)(2,1)S(1)}, u32[]{:S(2)}, u32[]{:S(2)}) collective-permute-start(bf16[10,2048]{1,0:T(8,128)(2,1)S(1)} %collective-permute-done.8), channel_id=1, source_target_pairs={{0,1},{1,2},{2,3},{3,4},{4,5},{5,6},{6,7},{7,8},{8,9},{9,10},{10,1... | collective-permute-start | bytes 122888 | tf_op jit(solution)/shard_map/ppermute | solution.py:117
  57.5 6.4 %collective-permute-start.16 = (bf16[10,2048]{1,0:T(8,128)(2,1)S(1)}, bf16[10,2048]{1,0:T(8,128)(2,1)S(1)}, u32[]{:S(2)}, u32[]{:S(2)}) collective-permute-start(bf16[10,2048]{1,0:T(8,128)(2,1)S(1)} %collective-permute-done.15), channel_id=1, source_target_pairs={{1,0},{2,1},{3,2},{4,3},{5,4},{6,5},{7,6},{8,7},{9,8},{10,9},{11,1... | collective-permute-start | bytes 122888 | tf_op jit(solution)/shard_map/ppermute | solution.py:119
  62.8 6.5 %collective-permute-start.10 = (bf16[10,2048]{1,0:T(8,128)(2,1)S(1)}, bf16[10,2048]{1,0:T(8,128)(2,1)S(1)}, u32[]{:S(2)}, u32[]{:S(2)}) collective-permute-start(bf16[10,2048]{1,0:T(8,128)(2,1)S(1)} %collective-permute-done.9), channel_id=1, source_target_pairs={{0,1},{1,2},{2,3},{3,4},{4,5},{5,6},{6,7},{7,8},{8,9},{9,10},{10,1... | collective-permute-start | bytes 122888 | tf_op jit(solution)/shard_map/ppermute | solution.py:117
  63.3 15.0 %copy-start.7 = (bf16[10,2048]{1,0:T(8,128)(2,1)S(1)}, bf16[10,2048]{1,0:T(8,128)(2,1)}, u32[]{:S(2)}) copy-start(bf16[10,2048]{1,0:T(8,128)(2,1)} %copy-done.6) | copy-start | bytes 122884
  63.9 6.4 %collective-permute-start.17 = (bf16[10,2048]{1,0:T(8,128)(2,1)S(1)}, bf16[10,2048]{1,0:T(8,128)(2,1)S(1)}, u32[]{:S(2)}, u32[]{:S(2)}) collective-permute-start(bf16[10,2048]{1,0:T(8,128)(2,1)S(1)} %collective-permute-done.16), channel_id=1, source_target_pairs={{1,0},{2,1},{3,2},{4,3},{5,4},{6,5},{7,6},{8,7},{9,8},{10,9},{11,1... | collective-permute-start | bytes 122888 | tf_op jit(solution)/shard_map/ppermute | solution.py:119
  69.3 6.5 %collective-permute-start.11 = (bf16[10,2048]{1,0:T(8,128)(2,1)S(1)}, bf16[10,2048]{1,0:T(8,128)(2,1)S(1)}, u32[]{:S(2)}, u32[]{:S(2)}) collective-permute-start(bf16[10,2048]{1,0:T(8,128)(2,1)S(1)} %collective-permute-done.10), channel_id=1, source_target_pairs={{0,1},{1,2},{2,3},{3,4},{4,5},{5,6},{6,7},{7,8},{8,9},{9,10},{10,1... | collective-permute-start | bytes 122888 | tf_op jit(solution)/shard_map/ppermute | solution.py:117
  70.3 9.0 %collective-permute-start.18 = (bf16[10,2048]{1,0:T(8,128)(2,1)S(1)}, bf16[10,2048]{1,0:T(8,128)(2,1)S(1)}, u32[]{:S(2)}, u32[]{:S(2)}) collective-permute-start(bf16[10,2048]{1,0:T(8,128)(2,1)S(1)} %collective-permute-done.17), channel_id=1, source_target_pairs={{1,0},{2,1},{3,2},{4,3},{5,4},{6,5},{7,6},{8,7},{9,8},{10,9},{11,1... | collective-permute-start | bytes 122888 | tf_op jit(solution)/shard_map/ppermute | solution.py:119
  80.1 21.0 %copy-start.4 = (f32[49,16,128]{2,1,0:T(8,128)S(1)}, f32[49,16,128]{2,1,0:T(8,128)}, u32[]{:S(2)}) copy-start(f32[49,16,128]{2,1,0:T(8,128)} %fusion.22) | copy-start | bytes 1204228
  86.2 14.8 %copy-start.2 = (f32[50,16,128]{2,1,0:T(8,128)S(1)}, f32[50,16,128]{2,1,0:T(8,128)}, u32[]{:S(2)}) copy-start(f32[50,16,128]{2,1,0:T(8,128)} %copy-done.1) | copy-start | bytes 1228804
  86.2 14.8 %copy-start.3 = (f32[50,16,128]{2,1,0:T(8,128)S(1)}, f32[50,16,128]{2,1,0:T(8,128)}, u32[]{:S(2)}) copy-start(f32[50,16,128]{2,1,0:T(8,128)} %param.15) | copy-start | bytes 1228804
  97.6 10.1 %all-to-all-start = ((bf16[10,16,16]{2,0,1:T(8,128)(2,1)}), bf16[10,16,16]{2,0,1:T(8,128)(2,1)S(1)}, u32[]{:S(2)}, u32[]{:S(2)}) async-start(bf16[10,16,16]{2,0,1:T(8,128)(2,1)} %pad_maximum_fusion.3), calls=%async_computation | async-start | bytes 131072 | tf_op jit(solution)/shard_map/all_to_all | solution.py:128
  101.1 6.7 %copy-start.10 = (s32[16,128]{1,0:T(8,128)S(1)}, s32[16,128]{1,0:T(8,128)}, u32[]{:S(2)}) copy-start(s32[16,128]{1,0:T(8,128)} %multiply_add_fusion) | copy-start | bytes 24580
  101.1 6.7 %copy-start.14 = (s32[256]{0:T(256)S(1)}, s32[256]{0:T(256)}, u32[]{:S(2)}) copy-start(s32[256]{0:T(256)} %and_select_fusion) | copy-start | bytes 3076
  102.7 5.6 %copy-start.8 = (f32[16,128]{1,0:T(8,128)S(1)}, f32[16,128]{1,0:T(8,128)}, u32[]{:S(2)}) copy-start(f32[16,128]{1,0:T(8,128)} %convert_element_type.30) | copy-start | bytes 24580
